TPU v7x, 32 devices: a whole 2x2x4 slice. The times are simulated.
32 devices in a mesh: blk: 8 (over z, core), seq: 4 (over y, x).
Axes of the slice: x: 2, y: 2, z: 4, core: 2. Of those that a mesh axis runs over, the one named last changes fastest.
Arguments:
- activations: bfloat16 [8, 2048, 8192], P('blk', 'seq'), may hold values from -6 to 6
- base_weight: bfloat16 [8192, 1024], P('blk', 'seq'), may hold values from -0.0625 to 0.0625
- adapter_down: bfloat16 [8, 16, 8192], P('blk'), may hold values from -0.0625 to 0.0625
- adapter_up: bfloat16 [8, 16, 1024], P('blk'), may hold values from -1.5 to 1.5
- cotangent: bfloat16 [8, 2048, 1024], P('blk', 'seq'), may hold values from -12 to 12
Outputs:
- projected: bfloat16 [8, 2048, 1024], P('blk', 'seq')
- gradient_inputs: bfloat16 [8, 2048, 8192], P('blk', 'seq')
- down_gradient: float32 [8, 16, 8192], P('blk')
- up_gradient: float32 [8, 16, 1024], P('blk')
All inputs are finite; a program needn't handle non-finite values.
Results may differ from a plain program's by a relative error of at most 0.0047.
Values may be sent and summed in bfloat16 or wider, within the bound.
No kernel may reach another device: no remote copies, remote signals or barrier semaphores. Data moves between devices by JAX's collectives and lax.ppermute only.
A program may use at most 128 MiB of HBM per device.

v0:
```python
import jax
import jax.numpy as jnp
from jax import lax
from jax.sharding import PartitionSpec as P

adapter_scale = 2.0


def body(activations, base_weight, adapter_down, adapter_up, cotangent):
    token_inputs = activations[0]
    down_matrix = adapter_down[0]
    up_matrix = adapter_up[0]
    output_cotangent = cotangent[0]
    token_count = token_inputs.shape[0] * lax.axis_size("seq")
    panel = lax.all_gather(base_weight, "seq", axis=1, tiled=True)
    lowrank_forward = jnp.dot(
        token_inputs, down_matrix.T, preferred_element_type=jnp.float32
    ).astype(jnp.bfloat16)
    lowrank_backward = jnp.dot(
        output_cotangent, up_matrix.T, preferred_element_type=jnp.float32
    ).astype(jnp.bfloat16)
    frozen_keys = jnp.dot(
        token_inputs,
        lax.all_gather(panel, "blk", axis=0, tiled=True),
        preferred_element_type=jnp.float32,
    )
    frozen_gradient = lax.dot_general(
        output_cotangent,
        lax.all_gather(panel, "blk", axis=0, tiled=True),
        (((1,), (1,)), ((), ())),
        preferred_element_type=jnp.float32,
    )
    projected = frozen_keys + adapter_scale * jnp.dot(
        lowrank_forward, up_matrix, preferred_element_type=jnp.float32
    )
    gradient_inputs = frozen_gradient + adapter_scale * jnp.dot(
        lowrank_backward, down_matrix, preferred_element_type=jnp.float32
    )
    local_down = jnp.dot(lowrank_backward.T, token_inputs, preferred_element_type=jnp.float32)
    local_up = jnp.dot(lowrank_forward.T, output_cotangent, preferred_element_type=jnp.float32)
    sum_down, sum_up = lax.psum((local_down, local_up), "seq")
    scale_factor = adapter_scale / token_count
    return (
        projected.astype(jnp.bfloat16)[None],
        gradient_inputs.astype(jnp.bfloat16)[None],
        (scale_factor * sum_down)[None],
        (scale_factor * sum_up)[None],
    )


def solution(mesh):
    return jax.shard_map(
        body,
        mesh=mesh,
        in_specs=(
            P("blk", "seq", None),
            P("blk", "seq"),
            P("blk", None, None),
            P("blk", None, None),
            P("blk", "seq", None),
        ),
        out_specs=(
            P("blk", "seq", None),
            P("blk", "seq", None),
            P("blk", None, None),
            P("blk", None, None),
        ),
        check_vma=False,
    )
```

profile of v0, /device:TPU:0, one launch (start us, length us, event | category | flops | bytes accessed | tf_op | source)
XLA Modules:
  0.0 299.8 jit_solution(208566958700023274)
XLA Ops:
  7.2 0.0 copy-start
  7.2 0.0 all-gather.3.cloned.1.call-start
  7.2 0.7 all-gather.3.cloned.1.call-update
  7.9 0.0 all-reduce.3.cloned.1.call-start
  8.0 0.4 copy-done
  8.4 0.0 copy-start.1
  8.4 1.3 convolution_convert_fusion
  9.7 6.0 %fusion.12 = bf16[512,16]{0,1:T(8,128)(2,1)S(1)} fusion(bf16[1,512,8192]{2,1,0:T(8,128)(2,1)} %param.5, bf16[1,16,8192]{2,1,0:T(8,128)(2,1)} %param.7), kind=kOutput, calls=%fused_computation.10 | convolution fusion | flops 134225920 | bytes 8667136 | tf_op jit(solution)/shard_map/dot_general | solution.py:16
  15.6 0.0 copy-start.3
  15.6 0.9 fusion.15
  16.5 0.0 copy-done.1
  16.6 2.0 fusion.1
  18.6 0.0 all-reduce.3.cloned.1.call-update
  18.6 0.2 all-gather.5.cloned.1.call-start
  18.8 28.9 %all-gather.3.cloned.1.call-done = bf16[1024,1024]{1,0:T(8,128)(2,1)} async-done(((bf16[1024,256]{1,0:T(8,128)(2,1)}), bf16[1024,1024]{1,0:T(8,128)(2,1)}) %all-gather.3.cloned.1.call-update) | async-done | bytes 2097168 | tf_op jit(solution)/shard_map/all_gather | solution.py:15
  47.7 0.0 all-gather.5.cloned.1.call-update
  47.8 0.0 copy-done.3
  47.8 0.5 fusion.23
  48.2 49.4 %all-reduce.3.cloned.1.call-done = (f32[16,8192]{1,0:T(8,128)}, f32[16,1024]{1,0:T(8,128)}) async-done(((f32[16,8192]{1,0:T(8,128)}, f32[16,1024]{1,0:T(8,128)}), (f32[16,8192]{1,0:T(8,128)}, f32[16,1024]{1,0:T(8,128)})) %all-reduce.3.cloned.1.call-update) | async-done | bytes 589840 | tf_op jit(solution)/shard_map/psum | solution.py:41
  97.6 1.5 multiply_bitcast_fusion.1
  99.1 1.9 multiply_bitcast_fusion
  100.9 0.0 copy-start.2
  100.9 149.5 %all-gather.5.cloned.1.call-done = bf16[8192,1024]{1,0:T(8,128)(2,1)} async-done(((bf16[1024,1024]{1,0:T(8,128)(2,1)}), bf16[8192,1024]{1,0:T(8,128)(2,1)}) %all-gather.5.cloned.1.call-update) | async-done | bytes 16777232 | tf_op jit(solution)/shard_map/all_gather | solution.py:24
  250.4 15.8 %fusion.18 = f32[512,8192]{1,0:T(8,128)} fusion(bf16[8192,1024]{1,0:T(8,128)(2,1)} %all-gather.5.cloned.1.call-done, bf16[1,512,1024]{2,1,0:T(8,128)(2,1)S(1)} %copy-done), kind=kOutput, calls=%fused_computation.15 | convolution fusion | flops 8589934592 | bytes 34603008 | tf_op jit(solution)/shard_map/dot_general | solution.py:27
  266.2 0.0 copy-done.2
  266.2 11.5 %fusion = bf16[1,512,8192]{2,1,0:T(8,128)(2,1)} fusion(f32[512,8192]{1,0:T(8,128)} %fusion.18, bf16[512,16]{0,1:T(8,128)(2,1)S(1)} %convolution_convert_fusion, bf16[1,16,8192]{2,1,0:T(8,128)(2,1)S(1)} %copy-done.2), kind=kOutput, calls=%fused_computation.1 | convolution fusion | flops 146800640 | bytes 25444352 | tf_op jit(solution)/shard_map/dot_general | solution.py:36
  277.7 15.5 %fusion.9 = bf16[1,512,1024]{2,1,0:T(8,128)(2,1)} fusion(f32[512,1024]{1,0:T(8,128)S(1)} %fusion.23, bf16[8192,1024]{1,0:T(8,128)(2,1)} %all-gather.5.cloned.1.call-done, bf16[1,512,8192]{2,1,0:T(8,128)(2,1)} %param.5), kind=kOutput, calls=%fused_computation.9 | convolution fusion | flops 8591507456 | bytes 28311552 | tf_op jit(solution)/shard_map/dot_general | solution.py:22
Async XLA Ops:
  7.2 1.2 copy-start
  7.2 40.6 %all-gather.3.cloned.1.call-start = ((), (), s32[]{:S(2)}) async-start(), calls=%async_computation | async-start | bytes 2621440 | tf_op jit(solution)/shard_map/all_gather | solution.py:15
  7.9 89.7 %all-reduce.3.cloned.1.call-start = ((), (), s32[]{:S(2)}) async-start(), calls=%async_computation.2 | async-start | bytes 1179648 | tf_op jit(solution)/shard_map/psum | solution.py:41
  8.4 8.2 %copy-start.1 = (bf16[1,512,8192]{2,1,0:T(8,128)(2,1)S(1)}, bf16[1,512,8192]{2,1,0:T(8,128)(2,1)}, u32[]{:S(2)}) copy-start(bf16[1,512,8192]{2,1,0:T(8,128)(2,1)} %param.5) | copy-start | bytes 25165828
  15.6 32.1 %copy-start.3 = (bf16[1,16,1024]{2,1,0:T(8,128)(2,1)S(1)}, bf16[1,16,1024]{2,1,0:T(8,128)(2,1)}, u32[]{:S(2)}) copy-start(bf16[1,16,1024]{2,1,0:T(8,128)(2,1)} %param.8) | copy-start | bytes 98308
  18.6 231.8 %all-gather.5.cloned.1.call-start = ((), (), s32[]{:S(2)}) async-start(), calls=%async_computation.1 | async-start | bytes 18874368 | tf_op jit(solution)/shard_map/all_gather | solution.py:24
  100.9 165.3 %copy-start.2 = (bf16[1,16,8192]{2,1,0:T(8,128)(2,1)S(1)}, bf16[1,16,8192]{2,1,0:T(8,128)(2,1)}, u32[]{:S(2)}) copy-start(bf16[1,16,8192]{2,1,0:T(8,128)(2,1)} %param.7) | copy-start | bytes 786436
Sparse Core Ops, SparseCore 0:
  9.8 37.8 all-gather.2
  51.3 46.2 all-reduce.2
  99.3 151.0 all-gather.4
where the time goes:
time: 300 us
  waiting for transfers between devices  228 us (76%)
  matrix products  53.4 us (18%)
  between operations  13.8 us (5%)
  other arithmetic  3.34 us (1%)
    all_gather x1, waiting for transfers between devices, body(): lax.all_gather(panel, 'blk', axis=0, tiled=True)  149 us
    psum x1, waiting for transfers between devices, body(): sum_down, sum_up = lax.psum((local_down, local_up), 'seq')  49.4 us
    all_gather x1, waiting for transfers between devices, body(): panel = lax.all_gather(base_weight, 'seq', axis=1, tiled=True)  28.9 us
    dot_general x1, matrix products, body(): lax.dot_general(output_cotangent, lax.all_gather(panel, 'blk', axis=0, ti...  15.8 us
    dot_general x1, matrix products, body(): jnp.dot(token_inputs, lax.all_gather(panel, 'blk', axis=0, tiled=True), p...  15.5 us
    dot_general x1, matrix products, body(): jnp.dot(lowrank_backward, down_matrix, preferred_element_type=jnp.float32)  11.5 us
  transfers between devices with their start and end apart: 3, of which 3 were waited for; matrix products, arithmetic and copies ran while one was open for 5% of the time, Pallas kernels for 0%

commit v1 on v0

--- a/solution.py
+++ b/solution.py
@@ -12,7 +12,12 @@
     up_matrix = adapter_up[0]
     output_cotangent = cotangent[0]
     token_count = token_inputs.shape[0] * lax.axis_size("seq")
-    panel = lax.all_gather(base_weight, "seq", axis=1, tiled=True)
+    ring = [base_weight]
+    for hop in range(3):
+        ring.append(lax.ppermute(ring[-1], "seq", [(dev, (dev + 1) % 4) for dev in range(4)]))
+    panel = jnp.roll(
+        jnp.concatenate(ring[::-1], axis=1), (lax.axis_index("seq") + 1) * ring[0].shape[1], axis=1
+    )
     lowrank_forward = jnp.dot(
         token_inputs, down_matrix.T, preferred_element_type=jnp.float32
     ).astype(jnp.bfloat16)

time: 300 us -> 265 us (0.88)
  waiting for transfers between devices: 228 us -> 172 us
  local copies, waits for them, and re-layouts: 0.45 us -> 16.3 us
  starting transfers between devices: 0.3 us -> 3.86 us
    all_gather x1, waiting for transfers between devices: 149 us -> 114 us  [body(): lax.all_gather(panel, 'blk', axis=0, tiled=True)]
    ppermute x0 -> x3, waiting for transfers between devices: none -> 32.1 us  [body(): lax.ppermute(ring[-1], 'seq', [(dev, (dev + 1) % 4) for dev in range(4)])]
    all_gather x1 -> x0, waiting for transfers between devices: 28.9 us -> none  [body(): panel = lax.all_gather(base_weight, 'seq', axis=1, tiled=True)]
    psum x1, waiting for transfers between devices: 49.4 us -> 25.4 us  [body(): sum_down, sum_up = lax.psum((local_down, local_up), 'seq')]
    unnamed x8 -> x21, local copies, waits for them, and re-layouts: 0.45 us -> 14.7 us
    ppermute x0 -> x3, starting transfers between devices: none -> 3.78 us  [body(): lax.ppermute(ring[-1], 'seq', [(dev, (dev + 1) % 4) for dev in range(4)])]
    dot_general x1, matrix products: 15.8 us -> 19.4 us  [body(): lax.dot_general(output_cotangent, lax.all_gather(panel, 'blk', axis=0, ti...]
  transfers between devices with their start and end apart: 3 -> 5, of which waited for: 3 -> 5; matrix products, arithmetic and copies ran while one was open for 5% -> 9% of each run, Pallas kernels for 0% -> 0%
where the time goes in v1:
time: 265 us; the launch traced here: 264 us
  waiting for transfers between devices  172 us (65%)
  matrix products  53.3 us (20%)
  local copies, waits for them, and re-layouts  16.3 us (6%)
  between operations  15.6 us (6%)
  starting transfers between devices  3.86 us (1%)
  other arithmetic  3.34 us (1%)
    all_gather x1, waiting for transfers between devices, body(): lax.all_gather(panel, 'blk', axis=0, tiled=True)  114 us
    ppermute x3, waiting for transfers between devices, body(): lax.ppermute(ring[-1], 'seq', [(dev, (dev + 1) % 4) for dev in range(4)])  32.1 us
    psum x1, waiting for transfers between devices, body(): sum_down, sum_up = lax.psum((local_down, local_up), 'seq')  25.4 us
    dot_general x1, matrix products, body(): lax.dot_general(output_cotangent, lax.all_gather(panel, 'blk', axis=0, ti...  19.4 us
    dot_general x1, matrix products, body(): jnp.dot(token_inputs, lax.all_gather(panel, 'blk', axis=0, tiled=True), p...  15.8 us
    unnamed x21, local copies, waits for them, and re-layouts  14.7 us
    dot_general x1, matrix products, body(): jnp.dot(lowrank_backward, down_matrix, preferred_element_type=jnp.float32)  8.79 us
    dot_general x1, matrix products, body(): jnp.dot(token_inputs, down_matrix.T, preferred_element_type=jnp.float32)  5.64 us
  transfers between devices with their start and end apart: 5, of which 5 were waited for; matrix products, arithmetic and copies ran while one was open for 9% of the time, Pallas kernels for 0%

profile of v1, /device:TPU:0, one launch (start us, length us, event | category | flops | bytes accessed | tf_op | source)
XLA Modules:
  0.0 264.4 jit_solution(2649256183257595832)
XLA Ops:
  8.0 0.0 copy-start
  8.0 0.0 copy-start.5
  8.0 0.0 all-reduce.3.cloned.1.call-start
  8.1 0.0 copy-start.2
  8.1 3.0 %collective-permute-start = (bf16[1024,256]{1,0:T(8,128)(2,1)}, bf16[1024,256]{1,0:T(8,128)(2,1)S(1)}, u32[]{:S(2)}, u32[]{:S(2)}) collective-permute-start(bf16[1024,256]{1,0:T(8,128)(2,1)} %param.6), channel_id=1, source_target_pairs={{0,1},{1,2},{2,3},{3,0},{4,5},{5,6},{6,7},{7,4},{8,9},{9,10},{10,1... | collective-permute-start | bytes 1572872 | tf_op jit(solution)/shard_map/ppermute | solution.py:17
  11.1 13.1 %collective-permute-done = bf16[1024,256]{1,0:T(8,128)(2,1)S(1)} collective-permute-done((bf16[1024,256]{1,0:T(8,128)(2,1)}, bf16[1024,256]{1,0:T(8,128)(2,1)S(1)}, u32[]{:S(2)}, u32[]{:S(2)}) %collective-permute-start) | collective-permute-done | bytes 524320 | tf_op jit(solution)/shard_map/ppermute | solution.py:17
  24.2 0.8 collective-permute-start.1
  24.9 5.6 %fusion.14 = bf16[512,16]{0,1:T(8,128)(2,1)S(1)} fusion(bf16[1,512,8192]{2,1,0:T(8,128)(2,1)} %param.5, bf16[1,16,8192]{2,1,0:T(8,128)(2,1)} %param.7), kind=kOutput, calls=%fused_computation.12 | convolution fusion | flops 134225920 | bytes 8667136 | tf_op jit(solution)/shard_map/dot_general | solution.py:21
  30.6 0.0 copy-done
  30.6 0.0 copy-done.5
  30.6 0.4 convolution_convert_fusion
  31.0 0.9 fusion.17
  31.9 0.0 copy-start.3
  31.9 6.3 %collective-permute-done.1 = bf16[1024,256]{1,0:T(8,128)(2,1)S(1)} collective-permute-done((bf16[1024,256]{1,0:T(8,128)(2,1)S(1)}, bf16[1024,256]{1,0:T(8,128)(2,1)S(1)}, u32[]{:S(2)}, u32[]{:S(2)}) %collective-permute-start.1) | collective-permute-done | bytes 524320 | tf_op jit(solution)/shard_map/ppermute | solution.py:17
  38.2 0.0 collective-permute-start.2
  38.2 0.0 copy-done.2
  38.2 2.0 fusion.2
  40.2 0.0 all-reduce.3.cloned.1.call-update
  40.2 0.0 all-gather.2.cloned.1.call-start
  40.3 12.7 %collective-permute-done.2 = bf16[1024,256]{1,0:T(8,128)(2,1)S(1)} collective-permute-done((bf16[1024,256]{1,0:T(8,128)(2,1)S(1)}, bf16[1024,256]{1,0:T(8,128)(2,1)S(1)}, u32[]{:S(2)}, u32[]{:S(2)}) %collective-permute-start.2) | collective-permute-done | bytes 524320 | tf_op jit(solution)/shard_map/ppermute | solution.py:17
  53.0 0.1 constant_dynamic-update-slice_fusion.7
  53.1 0.1 constant_dynamic-update-slice_fusion.6
  53.2 0.1 constant_dynamic-update-slice_fusion.5
  53.2 0.0 copy-done.3
  53.2 0.1 constant_dynamic-update-slice_fusion.4
  53.3 0.1 constant_dynamic-update-slice_fusion.3
  53.4 0.1 constant_dynamic-update-slice_fusion.2
  53.5 0.1 constant_dynamic-update-slice_fusion.1
  53.5 0.1 constant_dynamic-update-slice_fusion
  53.6 0.0 copy-start.4
  53.6 1.5 constant_dynamic-slice_fusion
  55.2 0.0 all-gather.2.cloned.1.call-update
  55.2 0.5 fusion.25
  55.7 0.0 copy-done.4
  55.7 8.8 %fusion.21 = f32[512,8192]{0,1:T(8,128)} fusion(bf16[512,16]{0,1:T(8,128)(2,1)S(1)} %convolution_convert_fusion, bf16[1,16,8192]{2,1,0:T(8,128)(2,1)S(1)} %copy-done.4), kind=kOutput, calls=%fused_computation.19 | convolution fusion | flops 134217728 | bytes 17055744 | tf_op jit(solution)/shard_map/dot_general | solution.py:41
  64.5 25.4 %all-reduce.3.cloned.1.call-done = (f32[16,8192]{1,0:T(8,128)}, f32[16,1024]{1,0:T(8,128)}) async-done(((f32[16,8192]{1,0:T(8,128)}, f32[16,1024]{1,0:T(8,128)}), (f32[16,8192]{1,0:T(8,128)}, f32[16,1024]{1,0:T(8,128)})) %all-reduce.3.cloned.1.call-update) | async-done | bytes 589840 | tf_op jit(solution)/shard_map/psum | solution.py:46
  89.9 1.5 multiply_bitcast_fusion.1
  91.3 1.9 multiply_bitcast_fusion
  93.2 114.4 %all-gather.2.cloned.1.call-done = bf16[8192,1024]{1,0:T(8,128)(2,1)} async-done(((bf16[1024,1024]{1,0:T(8,128)(2,1)}), bf16[8192,1024]{1,0:T(8,128)(2,1)}) %all-gather.2.cloned.1.call-update) | async-done | bytes 16777232 | tf_op jit(solution)/shard_map/all_gather | solution.py:29
  207.6 19.4 %fusion.1 = bf16[1,512,8192]{1,2,0:T(8,128)(2,1)} fusion(f32[512,8192]{0,1:T(8,128)} %fusion.21, bf16[8192,1024]{1,0:T(8,128)(2,1)} %all-gather.2.cloned.1.call-done, bf16[1,512,1024]{2,1,0:T(8,128)(2,1)S(1)} %copy-done), kind=kOutput, calls=%fused_computation.2 | convolution fusion | flops 8602517504 | bytes 42991616 | tf_op jit(solution)/shard_map/dot_general | solution.py:32
  227.0 11.9 %copy.12 = bf16[1,512,8192]{2,1,0:T(8,128)(2,1)} copy(bf16[1,512,8192]{1,2,0:T(8,128)(2,1)} %fusion.1) | data formatting | bytes 16777216
  238.9 0.0 copy-start.1
  238.9 15.8 %fusion.11 = bf16[1,512,1024]{1,2,0:T(8,128)(2,1)} fusion(f32[512,1024]{0,1:T(8,128)S(1)} %fusion.25, bf16[8192,1024]{1,0:T(8,128)(2,1)} %all-gather.2.cloned.1.call-done, bf16[1,512,8192]{2,1,0:T(8,128)(2,1)} %param.5), kind=kOutput, calls=%fused_computation.11 | convolution fusion | flops 8591507456 | bytes 28311552 | tf_op jit(solution)/shard_map/dot_general | solution.py:27
  254.7 2.3 copy.11
  257.0 0.0 copy-done.1
Async XLA Ops:
  8.0 22.6 %copy-start = (bf16[1,512,1024]{2,1,0:T(8,128)(2,1)S(1)}, bf16[1,512,1024]{2,1,0:T(8,128)(2,1)}, u32[]{:S(2)}) copy-start(bf16[1,512,1024]{2,1,0:T(8,128)(2,1)} %param.9) | copy-start | bytes 3145732
  8.0 22.6 %copy-start.5 = (bf16[1,16,1024]{2,1,0:T(8,128)(2,1)S(1)}, bf16[1,16,1024]{2,1,0:T(8,128)(2,1)}, u32[]{:S(2)}) copy-start(bf16[1,16,1024]{2,1,0:T(8,128)(2,1)} %param.8) | copy-start | bytes 98308
  8.0 81.8 %all-reduce.3.cloned.1.call-start = ((), (), s32[]{:S(2)}) async-start(), calls=%async_computation.1 | async-start | bytes 1179648 | tf_op jit(solution)/shard_map/psum | solution.py:46
  8.1 30.1 %copy-start.2 = (bf16[1,512,8192]{2,1,0:T(8,128)(2,1)S(1)}, bf16[1,512,8192]{2,1,0:T(8,128)(2,1)}, u32[]{:S(2)}) copy-start(bf16[1,512,8192]{2,1,0:T(8,128)(2,1)} %param.5) | copy-start | bytes 25165828
  8.1 16.1 %collective-permute-start = (bf16[1024,256]{1,0:T(8,128)(2,1)}, bf16[1024,256]{1,0:T(8,128)(2,1)S(1)}, u32[]{:S(2)}, u32[]{:S(2)}) collective-permute-start(bf16[1024,256]{1,0:T(8,128)(2,1)} %param.6), channel_id=1, source_target_pairs={{0,1},{1,2},{2,3},{3,0},{4,5},{5,6},{6,7},{7,4},{8,9},{9,10},{10,1... | collective-permute-start | bytes 1572872 | tf_op jit(solution)/shard_map/ppermute | solution.py:17
  24.2 14.0 %collective-permute-start.1 = (bf16[1024,256]{1,0:T(8,128)(2,1)S(1)}, bf16[1024,256]{1,0:T(8,128)(2,1)S(1)}, u32[]{:S(2)}, u32[]{:S(2)}) collective-permute-start(bf16[1024,256]{1,0:T(8,128)(2,1)S(1)} %collective-permute-done), channel_id=1, source_target_pairs={{0,1},{1,2},{2,3},{3,0},{4,5},{5,6},{6,7},{7,4},{8,9},{9,10},{10,1... | collective-permute-start | bytes 1572872 | tf_op jit(solution)/shard_map/ppermute | solution.py:17
  31.9 21.3 %copy-start.3 = (bf16[1024,256]{1,0:T(8,128)(2,1)S(1)}, bf16[1024,256]{1,0:T(8,128)(2,1)}, u32[]{:S(2)}) copy-start(bf16[1024,256]{1,0:T(8,128)(2,1)} %param.6) | copy-start | bytes 1572868
  38.2 14.8 %collective-permute-start.2 = (bf16[1024,256]{1,0:T(8,128)(2,1)S(1)}, bf16[1024,256]{1,0:T(8,128)(2,1)S(1)}, u32[]{:S(2)}, u32[]{:S(2)}) collective-permute-start(bf16[1024,256]{1,0:T(8,128)(2,1)S(1)} %collective-permute-done.1), channel_id=1, source_target_pairs={{0,1},{1,2},{2,3},{3,0},{4,5},{5,6},{6,7},{7,4},{8,9},{9,10},{10,1... | collective-permute-start | bytes 1572872 | tf_op jit(solution)/shard_map/ppermute | solution.py:17
  40.2 167.4 %all-gather.2.cloned.1.call-start = ((), (), s32[]{:S(2)}) async-start(), calls=%async_computation | async-start | bytes 18874368 | tf_op jit(solution)/shard_map/all_gather | solution.py:29
  53.6 2.1 copy-start.4
  238.9 18.0 %copy-start.1 = (bf16[1,512,1024]{2,1,0:T(8,128)(2,1)S(1)}, bf16[1,512,1024]{2,1,0:T(8,128)(2,1)}, u32[]{:S(2)}) copy-start(bf16[1,512,1024]{2,1,0:T(8,128)(2,1)} %param.9) | copy-start | bytes 3145732
Sparse Core Ops, SparseCore 0:
  40.3 49.4 all-reduce.2
Sparse Core Ops, SparseCore 1:
  55.3 152.3 all-gather.1
